TPU v7x, 32 devices: a whole 2x2x4 slice. The times are simulated.
32 devices in a mesh: macro: 4 (over y, x), micro: 8 (over z, core).
Axes of the slice: x: 2, y: 2, z: 4, core: 2. Of those that a mesh axis runs over, the one named last changes fastest.
Arguments:
- displacement: float32 [3, 8, 16, 256], P(None, 'macro', 'micro'), may hold values from -6 to 6
- load: float32 [3, 8, 16, 256], P(None, 'macro', 'micro'), may hold values from -6 to 6
- routes: int32 [4, 8, 1024, 1], P('macro', 'micro'), may hold values from 0 to 7; in each aligned block of 1024 rows (0 to 1023, 1024 to 2047, ..., all dimensions but the last counted through in order) at most 256 rows name the same one
- counts: int32 [4, 8, 1024], P('macro', 'micro'), may hold values from 1 to 4
- stiffness: bfloat16 [8, 512, 512], P('micro'), may hold values from -0.5 to 2.5, as said below
- precond: bfloat16 [8, 512, 512], P('micro'), may hold values from -0.5 to 2.5, as said below
- forcing: bfloat16 [8, 6, 512], P('micro'), may hold values from -2.5 to 2.5
- coupling: bfloat16 [8, 512, 6], P('micro'), may hold values from -0.25 to 0.25
- lame_first: float32 [8], P('micro'), may hold values from 0.5 to 2
- lame_shear: float32 [8], P('micro'), may hold values from 0.5 to 2
Outputs:
- increment: float32 [3, 8, 16, 256], P(None, 'macro', 'micro')
- residual: float32 [3, 8, 16, 256], P(None, 'macro', 'micro')
Inputs may be any that keep to these rules, and one draw needn't show every extreme that they name: `routes`: among the points of one block (one device's points), no owner is named by more than 256 points, a bound that some block reaches. `stiffness`: Symmetric. `precond`: Symmetric.
All inputs are finite; a program needn't handle non-finite values.
Results may differ from a plain program's by a relative error of at most 0.002.
Values sent between devices are 32-bit elements; how exact they have to be, the bound alone decides.
A program may use at most 64 MiB of HBM per device.

v0:
```python
import jax
import jax.numpy as jnp
from jax import lax
from jax.sharding import PartitionSpec as P

ITMAX = 4
ITERS = 5


BETA = 0.1
OMEGA = 0.8
MASS = 0.1
VOIGT = ((0, 5, 4), (5, 1, 3), (4, 3, 2))
ALL_PAIRS = tuple(
    ((first_axis, second_axis) for first_axis in range(6) for second_axis in range(6))
)


def with_halo(block, sides, width):
    for axis, dim in sides:
        count = lax.axis_size(axis)
        forward = [(i, i + 1) for i in range(count - 1)]
        backward = [(target, source) for source, target in forward]
        low = lax.ppermute(
            lax.slice_in_dim(block, block.shape[dim] - width, None, axis=dim), axis, forward
        )
        high = lax.ppermute(lax.slice_in_dim(block, 0, width, axis=dim), axis, backward)
        block = jnp.concatenate([low, block, high], axis=dim)
    return block


def passed_along(value, axis, steps):
    count = lax.axis_size(axis)
    initial, last = (max(0, -steps), min(count, count - steps))
    return lax.ppermute(value, axis, [(source, source + steps) for source in range(initial, last)])


def element_strain(nodes):
    count_x = nodes.shape[1] - 1
    count_y = nodes.shape[2] - 1
    count_z = nodes.shape[3]
    padded = jnp.pad(nodes, ((0, 0), (0, 0), (0, 0), (0, 1)))
    zeros = jnp.zeros((3, count_x, count_y, count_z), jnp.float32)
    grad_x, grad_y, grad_z = (zeros, zeros, zeros)
    for corner_x in (0, 1):
        for corner_y in (0, 1):
            for corner_z in (0, 1):
                piece = padded[
                    :,
                    corner_x : corner_x + count_x,
                    corner_y : corner_y + count_y,
                    corner_z : corner_z + count_z,
                ]
                grad_x = grad_x + 0.25 * (2 * corner_x - 1) * piece
                grad_y = grad_y + 0.25 * (2 * corner_y - 1) * piece
                grad_z = grad_z + 0.25 * (2 * corner_z - 1) * piece
    return jnp.stack(
        [
            grad_x[0],
            grad_y[1],
            grad_z[2],
            grad_z[1] + grad_y[2],
            grad_z[0] + grad_x[2],
            grad_y[0] + grad_x[1],
        ]
    )


def node_force(stress):
    count_x, count_y, count_z = (stress.shape[1], stress.shape[2], stress.shape[3])
    forces = jnp.zeros((3, count_x + 1, count_y + 1, count_z + 1), jnp.float32)
    for corner_x in (0, 1):
        for corner_y in (0, 1):
            for corner_z in (0, 1):
                signs = (2 * corner_x - 1, 2 * corner_y - 1, 2 * corner_z - 1)
                parts = []
                for component in range(3):
                    table = VOIGT[component]
                    parts.append(
                        0.25
                        * (
                            signs[0] * stress[table[0]]
                            + signs[1] * stress[table[1]]
                            + signs[2] * stress[table[2]]
                        )
                    )
                contrib = jnp.stack(parts)
                forces = forces + jnp.pad(
                    contrib,
                    (
                        (0, 0),
                        (corner_x, 1 - corner_x),
                        (corner_y, 1 - corner_y),
                        (corner_z, 1 - corner_z),
                    ),
                )
    return forces


def micro_solve(
    strain, sweeps, stiffness, precond, forcing, coupling, lame_first, lame_shear, pairs
):
    strain_half = strain.astype(jnp.bfloat16)
    modal_load = lax.dot_general(
        strain_half, forcing, (((0,), (0,)), ((), ())), preferred_element_type=jnp.float32
    )
    modes = jnp.zeros_like(modal_load)
    for sweep in range(ITMAX):
        misfit = (
            jnp.dot(modes.astype(jnp.bfloat16), stiffness, preferred_element_type=jnp.float32)
            + BETA * jnp.tanh(modes)
            - modal_load
        )
        update = modes - OMEGA * jnp.dot(
            misfit.astype(jnp.bfloat16), precond, preferred_element_type=jnp.float32
        )
        modes = jnp.where((sweeps[0] > sweep)[:, None], update, modes)
    trace = strain[0] + strain[1] + strain[2]
    elastic = jnp.stack(
        [
            lame_first * trace + 2.0 * lame_shear * strain[0],
            lame_first * trace + 2.0 * lame_shear * strain[1],
            lame_first * trace + 2.0 * lame_shear * strain[2],
            lame_shear * strain[3],
            lame_shear * strain[4],
            lame_shear * strain[5],
        ]
    )
    stress = elastic + lax.dot_general(
        coupling,
        modes.astype(jnp.bfloat16),
        (((0,), (1,)), ((), ())),
        preferred_element_type=jnp.float32,
    )
    slope = 1.0 - jnp.tanh(modes) ** 2
    wide = coupling.astype(jnp.float32)
    products = jnp.stack([wide[:, pair[0]] * wide[:, pair[1]] for pair in pairs], axis=1)
    extra = lax.dot_general(
        products,
        slope,
        (((0,), (1,)), ((), ())),
        precision=lax.Precision.HIGHEST,
        preferred_element_type=jnp.float32,
    )
    base = jnp.stack(
        [
            lame_first * float(pair[0] < 3 and pair[1] < 3)
            + lame_shear
            * (
                2.0 * float(pair[0] == pair[1] and pair[0] < 3)
                + float(pair[0] == pair[1] and pair[0] >= 3)
            )
            for pair in pairs
        ]
    )
    return jnp.concatenate([stress, extra + base[:, None]], axis=0)


def extend(field):
    return with_halo(field, (("macro", 1), ("micro", 2)), 1)


def operate(field, tangent_ext):
    strain = element_strain(extend(field))
    stress = jnp.sum(tangent_ext * strain[None], axis=1)
    return MASS * field + node_force(stress)[:, 1:-1, 1:-1, :-1]


def two_products(residual, image):
    return lax.psum((jnp.sum(residual * residual), jnp.sum(residual * image)), ("macro", "micro"))


def shards(
    displacement,
    load,
    routes,
    counts,
    stiffness,
    precond,
    forcing,
    coupling,
    lame_first,
    lame_shear,
):
    count_x, count_y, count_z = (
        displacement.shape[1],
        displacement.shape[2],
        displacement.shape[3],
    )
    points = count_x * count_y * count_z
    owners = lax.axis_size("micro")
    capacity = max(2, 2 * points // owners)
    strain_ext = element_strain(extend(displacement))
    strain_points = strain_ext[:, 1:, 1:].reshape(6, points)
    owner_of = routes.reshape(points)
    sweeps_of = counts.reshape(points)
    onehot = (owner_of[:, None] == jnp.arange(owners, dtype=jnp.int32)[None, :]).astype(jnp.int32)
    ranks = jnp.sum((jnp.cumsum(onehot, axis=0) - 1) * onehot, axis=1)
    target = owner_of * capacity + ranks
    send_strain = jnp.zeros((6, owners * capacity), jnp.float32).at[:, target].set(strain_points)
    send_sweeps = jnp.zeros((1, owners * capacity), jnp.int32).at[0, target].set(sweeps_of)
    got_strain, got_sweeps = (
        lax.all_to_all(send_strain, "micro", split_axis=1, concat_axis=1, tiled=True),
        lax.all_to_all(send_sweeps, "micro", split_axis=1, concat_axis=1, tiled=True),
    )
    rows = micro_solve(
        got_strain,
        got_sweeps,
        stiffness[0],
        precond[0],
        forcing[0],
        coupling[0],
        lame_first[0],
        lame_shear[0],
        ALL_PAIRS,
    )
    back = lax.all_to_all(rows, "micro", split_axis=1, concat_axis=1, tiled=True)
    values = jnp.take(back, target, axis=1)
    values = values.reshape(42, count_x, count_y, count_z)
    left_x = passed_along(values[:, -1:], "macro", 1)
    values = jnp.concatenate([left_x, values], axis=1)
    left_y = passed_along(values[:, :, -1:], "micro", 1)
    values = jnp.concatenate([left_y, values], axis=2)
    stress_ext = values[:6]
    tangent_ext = values[6:].reshape(6, 6, count_x + 1, count_y + 1, count_z)
    rhs = load - node_force(stress_ext)[:, 1:-1, 1:-1, :-1]

    def apply(field):
        return operate(field, tangent_ext)

    increment = jnp.zeros_like(rhs)
    residual = rhs
    image = apply(residual)
    norm_now, product = two_products(residual, image)
    alpha = norm_now / product
    direction, along = (residual, image)
    for step in range(ITERS):
        increment = increment + alpha * direction
        residual = residual - alpha * along
        if step + 1 < ITERS:
            image = apply(residual)
            norm_next, product = two_products(residual, image)
            ratio = norm_next / norm_now
            alpha = norm_next / (product - ratio * norm_next / alpha)
            direction = residual + ratio * direction
            along = image + ratio * along
            norm_now = norm_next
    return (increment, residual)


def solution(mesh):
    in_specs = (
        P(None, "macro", "micro", None),
        P(None, "macro", "micro", None),
        P("macro", "micro", None, None),
        P("macro", "micro", None),
        P("micro", None, None),
        P("micro", None, None),
        P("micro", None, None),
        P("micro", None, None),
        P("micro"),
        P("micro"),
    )
    out_specs = (P(None, "macro", "micro", None), P(None, "macro", "micro", None))
    return jax.shard_map(shards, mesh=mesh, in_specs=in_specs, out_specs=out_specs, check_vma=False)
```

profile of v0, /device:TPU:0, one launch (start us, length us, event | category | flops | bytes accessed | tf_op | source)
XLA Modules:
  0.0 446.3 jit_solution(9777166148011291204)
XLA Ops:
  1.4 4.9 %collective-permute-start = (f32[3,1,2,256]{3,2,1,0:T(2,128)S(1)}, f32[3,1,2,256]{3,2,1,0:T(2,128)S(1)}, u32[]{:S(2)}, u32[]{:S(2)}) collective-permute-start(f32[3,1,2,256]{3,2,1,0:T(2,128)S(1)} %get-tuple-element.267), channel_id=1, source_target_pairs={{0,8},{8,16},{16,24},{1,9},{9,17},{17,25},{2,10},{10,18},{18,26},{... | collective-permute-start | bytes 18440 | tf_op jit(solution)/shard_map/ppermute | solution.py:24
  14.0 5.0 %scatter_custom_fusion.1 = s32[2048]{0:T(1024)} fusion(s32[1024]{0:T(1024)S(1)} %broadcast_select_fusion.1, s32[1024]{0:T(1024)} %bitcast.117, s32[]{:T(128)} %constant.19.clone.1), kind=kCustom, calls=%fused_computation.834 | custom fusion | bytes 8704
  19.0 4.9 %all-to-all-start.1 = ((s32[1,8,256]{2,0,1:T(1,128)}), s32[1,8,256]{2,0,1:T(1,128)S(1)}, u32[]{:S(2)}, u32[]{:S(2)}) async-start(s32[1,8,256]{2,0,1:T(1,128)} %bitcast.18), calls=%async_computation.1 | async-start | bytes 16384 | tf_op jit(solution)/shard_map/all_to_all | solution.py:204
  32.9 3.3 scatter_custom_fusion
  37.2 5.7 %all-to-all-start = ((f32[6,8,256]{2,0,1:T(8,128)}), f32[6,8,256]{2,0,1:T(8,128)S(1)}, u32[]{:S(2)}, u32[]{:S(2)}) async-start(f32[6,8,256]{2,0,1:T(8,128)} %copy.26), calls=%async_computation | async-start | bytes 131072 | tf_op jit(solution)/shard_map/all_to_all | solution.py:203
  43.1 5.8 %all-to-all-done = f32[6,8,256]{2,0,1:T(8,128)S(1)} async-done(((f32[6,8,256]{2,0,1:T(8,128)}), f32[6,8,256]{2,0,1:T(8,128)S(1)}, u32[]{:S(2)}, u32[]{:S(2)}) %all-to-all-start) | async-done | bytes 49184 | tf_op jit(solution)/shard_map/all_to_all | solution.py:203
  51.6 6.6 %subtract_select_fusion.3 = f32[2048,512]{1,0:T(8,128)} fusion(pred[2048]{0:T(1024)(128)(4,1)S(1)} %gt.63, f32[2048,512]{1,0:T(8,128)} %fusion.206, bf16[1,512,512]{2,1,0:T(8,128)(2,1)S(1)} %copy-done, bf16[1,512,512]{2,1,0:T(8,128)(2,1)S(1)} %copy-done.6), kind=kOutput, calls=%fused_computation.13 | convolution fusion | flops 2152726528 | bytes 9439232 | tf_op jit(solution)/shard_map/dot_general | solution.py:114
  58.1 9.7 %subtract_select_fusion.2 = f32[2048,512]{1,0:T(8,128)} fusion(f32[2048,512]{1,0:T(8,128)} %subtract_select_fusion.3, pred[2048]{0:T(1024)(128)(4,1)S(1)} %gt.60, f32[2048,512]{1,0:T(8,128)} %fusion.206, bf16[1,512,512]{2,1,0:T(8,128)(2,1)S(1)} %copy-done, bf16[1,512,512]{2,1,0:T(8,128)(2,1)S(1)} %copy-done.6), kind=kOutput, calls=%fused_computation.5 | convolution fusion | flops 2155872256 | bytes 13633536 | tf_op jit(solution)/shard_map/dot_general | solution.py:114
  67.8 10.1 %subtract_select_fusion.1 = f32[2048,512]{1,0:T(8,128)} fusion(f32[2048,512]{1,0:T(8,128)} %subtract_select_fusion.2, pred[2048]{0:T(1024)(128)(4,1)S(1)} %gt.57, f32[2048,512]{1,0:T(8,128)} %fusion.206, bf16[1,512,512]{2,1,0:T(8,128)(2,1)S(1)} %copy-done, bf16[1,512,512]{2,1,0:T(8,128)(2,1)S(1)} %copy-done.6), kind=kOutput, calls=%fused_computation.4 | convolution fusion | flops 2155872256 | bytes 13633536 | tf_op jit(solution)/shard_map/dot_general | solution.py:114
  77.9 9.7 %subtract_select_fusion = f32[2048,512]{1,0:T(8,128)} fusion(f32[2048,512]{1,0:T(8,128)} %subtract_select_fusion.1, pred[2048]{0:T(1024)(128)(4,1)S(1)} %gt.54, f32[2048,512]{1,0:T(8,128)} %fusion.206, bf16[1,512,512]{2,1,0:T(8,128)(2,1)S(1)} %copy-done, bf16[1,512,512]{2,1,0:T(8,128)(2,1)S(1)} %copy-done.6), kind=kOutput, calls=%fused_computation.3 | convolution fusion | flops 2155872256 | bytes 13633536 | tf_op jit(solution)/shard_map/dot_general | solution.py:114
  87.8 3.0 fusion.7
  91.3 4.2 fusion.4
  96.6 3.6 all-to-all-start.2
  100.3 12.3 %all-to-all-done.2 = f32[42,8,256]{2,0,1:T(8,128)S(1)} async-done(((f32[42,8,256]{2,0,1:T(8,128)}), f32[42,8,256]{2,0,1:T(8,128)S(1)}, u32[]{:S(2)}, u32[]{:S(2)}) %all-to-all-start.2) | async-done | bytes 344096 | tf_op jit(solution)/shard_map/all_to_all | solution.py:217
  113.0 2.8 gather_fusion
  116.1 4.5 %collective-permute-start.4 = (f32[42,1,2,256]{3,2,1,0:T(2,128)S(1)}, f32[42,1,2,256]{3,2,1,0:T(2,128)S(1)}, u32[]{:S(2)}, u32[]{:S(2)}) collective-permute-start(f32[42,1,2,256]{3,2,1,0:T(2,128)S(1)} %slice.1305), channel_id=1, source_target_pairs={{0,8},{8,16},{16,24},{1,9},{9,17},{17,25},{2,10},{10,18},{18,26},{... | collective-permute-start | bytes 258056 | tf_op jit(solution)/shard_map/ppermute | solution.py:35
  126.1 4.3 collective-permute-start.6
  131.7 5.5 %collective-permute-done.7 = f32[3,1,2,256]{3,2,1,0:T(2,128)S(1)} collective-permute-done((f32[3,1,2,256]{3,2,1,0:T(2,128)S(1)}, f32[3,1,2,256]{3,2,1,0:T(2,128)S(1)}, u32[]{:S(2)}, u32[]{:S(2)}) %collective-permute-start.7) | collective-permute-done | bytes 6176 | tf_op jit(solution)/shard_map/ppermute | solution.py:27
  140.8 4.6 %collective-permute-done.9 = f32[3,4,1,256]{3,2,1,0:T(1,128)S(1)} collective-permute-done((f32[3,4,1,256]{3,2,1,0:T(1,128)S(1)}, f32[3,4,1,256]{3,2,1,0:T(1,128)S(1)}, u32[]{:S(2)}, u32[]{:S(2)}) %collective-permute-start.9) | collective-permute-done | bytes 12320 | tf_op jit(solution)/shard_map/ppermute | solution.py:27
  147.5 42.8 %all-reduce.59 = (f32[]{:T(128)}, f32[]{:T(128)}) all-reduce(f32[]{:T(128)} %get-tuple-element.11, f32[]{:T(128)} %get-tuple-element.10), channel_id=1, replica_groups=mesh['macro'=4,'micro'=8] {'macro','micro'}, use_global_device_ids=true, to_apply=%region_6.7 | all-reduce | flops 2 | bytes 16 | tf_op jit(solution)/shard_map/psum | solution.py:170
  191.6 4.2 collective-permute-start.10
  197.1 4.2 collective-permute-done.11
  208.7 42.4 %all-reduce.58 = (f32[]{:T(128)}, f32[]{:T(128)}) all-reduce(f32[]{:T(128)} %get-tuple-element.9, f32[]{:T(128)} %get-tuple-element.8), channel_id=1, replica_groups=mesh['macro'=4,'micro'=8] {'macro','micro'}, use_global_device_ids=true, to_apply=%region_11.12 | all-reduce | flops 2 | bytes 16 | tf_op jit(solution)/shard_map/psum | solution.py:170
  255.5 4.2 collective-permute-start.14
  261.0 4.2 collective-permute-done.15
  272.5 42.5 %all-reduce.57 = (f32[]{:T(128)}, f32[]{:T(128)}) all-reduce(f32[]{:T(128)} %get-tuple-element.7, f32[]{:T(128)} %get-tuple-element.6), channel_id=1, replica_groups=mesh['macro'=4,'micro'=8] {'macro','micro'}, use_global_device_ids=true, to_apply=%region_16.17 | all-reduce | flops 2 | bytes 16 | tf_op jit(solution)/shard_map/psum | solution.py:170
  318.8 4.2 collective-permute-start.18
  324.3 4.2 collective-permute-done.19
  335.9 42.4 %all-reduce.56 = (f32[]{:T(128)}, f32[]{:T(128)}) all-reduce(f32[]{:T(128)} %get-tuple-element.5, f32[]{:T(128)} %get-tuple-element.4), channel_id=1, replica_groups=mesh['macro'=4,'micro'=8] {'macro','micro'}, use_global_device_ids=true, to_apply=%region_21.22 | all-reduce | flops 2 | bytes 16 | tf_op jit(solution)/shard_map/psum | solution.py:170
  382.2 4.2 collective-permute-start.22
  387.8 4.2 collective-permute-done.23
  399.3 42.4 %all-reduce.55 = (f32[]{:T(128)}, f32[]{:T(128)}) all-reduce(f32[]{:T(128)} %get-tuple-element.3, f32[]{:T(128)} %get-tuple-element.2), channel_id=1, replica_groups=mesh['macro'=4,'micro'=8] {'macro','micro'}, use_global_device_ids=true, to_apply=%region_26.27 | all-reduce | flops 2 | bytes 16 | tf_op jit(solution)/shard_map/psum | solution.py:170
  (288 shorter events, 69.1 us)
Async XLA Ops:
  0.6 50.9 %copy-start = (bf16[1,512,512]{2,1,0:T(8,128)(2,1)S(1)}, bf16[1,512,512]{2,1,0:T(8,128)(2,1)}, u32[]{:S(2)}) copy-start(bf16[1,512,512]{2,1,0:T(8,128)(2,1)} %param.15) | copy-start | bytes 1572868
  0.6 48.2 %copy-start.5 = (bf16[1,6,512]{2,1,0:T(8,128)(2,1)S(1)}, bf16[1,6,512]{2,1,0:T(8,128)(2,1)}, u32[]{:S(2)}) copy-start(bf16[1,6,512]{2,1,0:T(8,128)(2,1)} %param.16) | copy-start | bytes 18436
  1.4 23.2 %collective-permute-start = (f32[3,1,2,256]{3,2,1,0:T(2,128)S(1)}, f32[3,1,2,256]{3,2,1,0:T(2,128)S(1)}, u32[]{:S(2)}, u32[]{:S(2)}) collective-permute-start(f32[3,1,2,256]{3,2,1,0:T(2,128)S(1)} %get-tuple-element.267), channel_id=1, source_target_pairs={{0,8},{8,16},{16,24},{1,9},{9,17},{17,25},{2,10},{10,18},{18,26},{... | collective-permute-start | bytes 18440 | tf_op jit(solution)/shard_map/ppermute | solution.py:24
  6.3 19.1 %collective-permute-start.1 = (f32[3,1,2,256]{3,2,1,0:T(2,128)S(1)}, f32[3,1,2,256]{3,2,1,0:T(2,128)S(1)}, u32[]{:S(2)}, u32[]{:S(2)}) collective-permute-start(f32[3,1,2,256]{3,2,1,0:T(2,128)S(1)} %get-tuple-element.266), channel_id=1, source_target_pairs={{8,0},{16,8},{24,16},{9,1},{17,9},{25,17},{10,2},{18,10},{26,18},{... | collective-permute-start | bytes 18440 | tf_op jit(solution)/shard_map/ppermute | solution.py:27
  19.0 18.2 %all-to-all-start.1 = ((s32[1,8,256]{2,0,1:T(1,128)}), s32[1,8,256]{2,0,1:T(1,128)S(1)}, u32[]{:S(2)}, u32[]{:S(2)}) async-start(s32[1,8,256]{2,0,1:T(1,128)} %bitcast.18), calls=%async_computation.1 | async-start | bytes 16384 | tf_op jit(solution)/shard_map/all_to_all | solution.py:204
  25.4 5.4 %collective-permute-start.2 = (f32[3,4,1,256]{3,2,1,0:T(1,128)S(1)}, f32[3,4,1,256]{3,2,1,0:T(1,128)S(1)}, u32[]{:S(2)}, u32[]{:S(2)}) collective-permute-start(f32[3,4,1,256]{3,2,1,0:T(1,128)S(1)} %get-tuple-element.226), channel_id=1, source_target_pairs={{0,1},{1,2},{2,3},{3,4},{4,5},{5,6},{6,7},{8,9},{9,10},{10,11},{11... | collective-permute-start | bytes 36872 | tf_op jit(solution)/shard_map/ppermute | solution.py:24
  27.8 4.2 collective-permute-start.3
  37.2 11.6 %all-to-all-start = ((f32[6,8,256]{2,0,1:T(8,128)}), f32[6,8,256]{2,0,1:T(8,128)S(1)}, u32[]{:S(2)}, u32[]{:S(2)}) async-start(f32[6,8,256]{2,0,1:T(8,128)} %copy.26), calls=%async_computation | async-start | bytes 131072 | tf_op jit(solution)/shard_map/all_to_all | solution.py:203
  96.6 29.3 %copy-start.4 = (f32[3,2,2,256]{3,2,1,0:T(2,128)S(1)}, f32[3,2,2,256]{3,2,1,0:T(2,128)}, u32[]{:S(2)}) copy-start(f32[3,2,2,256]{3,2,1,0:T(2,128)} %param.11) | copy-start | bytes 36868
  96.6 16.0 %all-to-all-start.2 = ((f32[42,8,256]{2,0,1:T(8,128)}), f32[42,8,256]{2,0,1:T(8,128)S(1)}, u32[]{:S(2)}, u32[]{:S(2)}) async-start(f32[42,8,256]{2,0,1:T(8,128)} %copy.27), calls=%async_computation.2 | async-start | bytes 786432 | tf_op jit(solution)/shard_map/all_to_all | solution.py:217
  116.1 6.6 %collective-permute-start.4 = (f32[42,1,2,256]{3,2,1,0:T(2,128)S(1)}, f32[42,1,2,256]{3,2,1,0:T(2,128)S(1)}, u32[]{:S(2)}, u32[]{:S(2)}) collective-permute-start(f32[42,1,2,256]{3,2,1,0:T(2,128)S(1)} %slice.1305), channel_id=1, source_target_pairs={{0,8},{8,16},{16,24},{1,9},{9,17},{17,25},{2,10},{10,18},{18,26},{... | collective-permute-start | bytes 258056 | tf_op jit(solution)/shard_map/ppermute | solution.py:35
  122.9 2.3 collective-permute-start.5
  126.1 5.6 %collective-permute-start.6 = (f32[3,1,2,256]{3,2,1,0:T(2,128)S(1)}, f32[3,1,2,256]{3,2,1,0:T(2,128)S(1)}, u32[]{:S(2)}, u32[]{:S(2)}) collective-permute-start(f32[3,1,2,256]{3,2,1,0:T(2,128)S(1)} %get-tuple-element.259), channel_id=1, source_target_pairs={{0,8},{8,16},{16,24},{1,9},{9,17},{17,25},{2,10},{10,18},{18,26},{... | collective-permute-start | bytes 18440 | tf_op jit(solution)/shard_map/ppermute | solution.py:24
  130.4 6.8 %collective-permute-start.7 = (f32[3,1,2,256]{3,2,1,0:T(2,128)S(1)}, f32[3,1,2,256]{3,2,1,0:T(2,128)S(1)}, u32[]{:S(2)}, u32[]{:S(2)}) collective-permute-start(f32[3,1,2,256]{3,2,1,0:T(2,128)S(1)} %get-tuple-element.260), channel_id=1, source_target_pairs={{8,0},{16,8},{24,16},{9,1},{17,9},{25,17},{10,2},{18,10},{26,18},{... | collective-permute-start | bytes 18440 | tf_op jit(solution)/shard_map/ppermute | solution.py:27
  137.2 3.5 collective-permute-start.8
  139.3 6.1 %collective-permute-start.9 = (f32[3,4,1,256]{3,2,1,0:T(1,128)S(1)}, f32[3,4,1,256]{3,2,1,0:T(1,128)S(1)}, u32[]{:S(2)}, u32[]{:S(2)}) collective-permute-start(f32[3,4,1,256]{3,2,1,0:T(1,128)S(1)} %get-tuple-element.224), channel_id=1, source_target_pairs={{1,0},{2,1},{3,2},{4,3},{5,4},{6,5},{7,6},{9,8},{10,9},{11,10},{12... | collective-permute-start | bytes 36872 | tf_op jit(solution)/shard_map/ppermute | solution.py:27
  191.6 5.5 %collective-permute-start.10 = (f32[3,1,2,256]{3,2,1,0:T(2,128)S(1)}, f32[3,1,2,256]{3,2,1,0:T(2,128)S(1)}, u32[]{:S(2)}, u32[]{:S(2)}) collective-permute-start(f32[3,1,2,256]{3,2,1,0:T(2,128)S(1)} %get-tuple-element.257), channel_id=1, source_target_pairs={{0,8},{8,16},{16,24},{1,9},{9,17},{17,25},{2,10},{10,18},{18,26},{... | collective-permute-start | bytes 18440 | tf_op jit(solution)/shard_map/ppermute | solution.py:24
  195.8 5.5 %collective-permute-start.11 = (f32[3,1,2,256]{3,2,1,0:T(2,128)S(1)}, f32[3,1,2,256]{3,2,1,0:T(2,128)S(1)}, u32[]{:S(2)}, u32[]{:S(2)}) collective-permute-start(f32[3,1,2,256]{3,2,1,0:T(2,128)S(1)} %get-tuple-element.258), channel_id=1, source_target_pairs={{8,0},{16,8},{24,16},{9,1},{17,9},{25,17},{10,2},{18,10},{26,18},{... | collective-permute-start | bytes 18440 | tf_op jit(solution)/shard_map/ppermute | solution.py:27
  201.4 2.6 collective-permute-start.12
  202.7 3.8 collective-permute-start.13
  255.5 5.5 %collective-permute-start.14 = (f32[3,1,2,256]{3,2,1,0:T(2,128)S(1)}, f32[3,1,2,256]{3,2,1,0:T(2,128)S(1)}, u32[]{:S(2)}, u32[]{:S(2)}) collective-permute-start(f32[3,1,2,256]{3,2,1,0:T(2,128)S(1)} %get-tuple-element.255), channel_id=1, source_target_pairs={{0,8},{8,16},{16,24},{1,9},{9,17},{17,25},{2,10},{10,18},{18,26},{... | collective-permute-start | bytes 18440 | tf_op jit(solution)/shard_map/ppermute | solution.py:24
  259.7 5.5 %collective-permute-start.15 = (f32[3,1,2,256]{3,2,1,0:T(2,128)S(1)}, f32[3,1,2,256]{3,2,1,0:T(2,128)S(1)}, u32[]{:S(2)}, u32[]{:S(2)}) collective-permute-start(f32[3,1,2,256]{3,2,1,0:T(2,128)S(1)} %get-tuple-element.256), channel_id=1, source_target_pairs={{8,0},{16,8},{24,16},{9,1},{17,9},{25,17},{10,2},{18,10},{26,18},{... | collective-permute-start | bytes 18440 | tf_op jit(solution)/shard_map/ppermute | solution.py:27
  265.2 2.6 collective-permute-start.16
  266.5 3.8 collective-permute-start.17
  318.8 5.5 %collective-permute-start.18 = (f32[3,1,2,256]{3,2,1,0:T(2,128)S(1)}, f32[3,1,2,256]{3,2,1,0:T(2,128)S(1)}, u32[]{:S(2)}, u32[]{:S(2)}) collective-permute-start(f32[3,1,2,256]{3,2,1,0:T(2,128)S(1)} %get-tuple-element.253), channel_id=1, source_target_pairs={{0,8},{8,16},{16,24},{1,9},{9,17},{17,25},{2,10},{10,18},{18,26},{... | collective-permute-start | bytes 18440 | tf_op jit(solution)/shard_map/ppermute | solution.py:24
  323.0 5.5 %collective-permute-start.19 = (f32[3,1,2,256]{3,2,1,0:T(2,128)S(1)}, f32[3,1,2,256]{3,2,1,0:T(2,128)S(1)}, u32[]{:S(2)}, u32[]{:S(2)}) collective-permute-start(f32[3,1,2,256]{3,2,1,0:T(2,128)S(1)} %get-tuple-element.254), channel_id=1, source_target_pairs={{8,0},{16,8},{24,16},{9,1},{17,9},{25,17},{10,2},{18,10},{26,18},{... | collective-permute-start | bytes 18440 | tf_op jit(solution)/shard_map/ppermute | solution.py:27
  328.6 2.6 collective-permute-start.20
  329.8 3.8 collective-permute-start.21
  382.2 5.5 %collective-permute-start.22 = (f32[3,1,2,256]{3,2,1,0:T(2,128)S(1)}, f32[3,1,2,256]{3,2,1,0:T(2,128)S(1)}, u32[]{:S(2)}, u32[]{:S(2)}) collective-permute-start(f32[3,1,2,256]{3,2,1,0:T(2,128)S(1)} %get-tuple-element.251), channel_id=1, source_target_pairs={{0,8},{8,16},{16,24},{1,9},{9,17},{17,25},{2,10},{10,18},{18,26},{... | collective-permute-start | bytes 18440 | tf_op jit(solution)/shard_map/ppermute | solution.py:24
  386.4 5.5 %collective-permute-start.23 = (f32[3,1,2,256]{3,2,1,0:T(2,128)S(1)}, f32[3,1,2,256]{3,2,1,0:T(2,128)S(1)}, u32[]{:S(2)}, u32[]{:S(2)}) collective-permute-start(f32[3,1,2,256]{3,2,1,0:T(2,128)S(1)} %get-tuple-element.252), channel_id=1, source_target_pairs={{8,0},{16,8},{24,16},{9,1},{17,9},{25,17},{10,2},{18,10},{26,18},{... | collective-permute-start | bytes 18440 | tf_op jit(solution)/shard_map/ppermute | solution.py:27
  392.0 2.6 collective-permute-start.24
  393.3 3.8 collective-permute-start.25
  (4 other events, 43.2 us)
where the time goes:
time: 449 us; the launch traced here: 446 us
  blocking collectives  212 us (47%)
  starting transfers between devices  71.2 us (16%)
  waiting for transfers between devices  59.1 us (13%)
  matrix products  46 us (10%)
  between operations  20.8 us (5%)
  other arithmetic  19.8 us (4%)
  local copies, waits for them, and re-layouts  17 us (4%)
    psum x5, blocking collectives, two_products(): lax.psum((jnp.sum(residual * residual), jnp.sum(residual * image)), ('mac...  212 us
    ppermute x12, waiting for transfers between devices, with_halo(): lax.ppermute(lax.slice_in_dim(block, 0, width, axis=dim), axis, backward)  38.2 us
    dot_general x4, matrix products, micro_solve(): jnp.dot(misfit.astype(jnp.bfloat16), precond, preferred_element_type=jnp....  36.1 us
    ppermute x12, starting transfers between devices, with_halo(): lax.ppermute(lax.slice_in_dim(block, block.shape[dim] - width, None, axis...  35.5 us
    ppermute x12, starting transfers between devices, with_halo(): lax.ppermute(lax.slice_in_dim(block, 0, width, axis=dim), axis, backward)  15.5 us
    all_to_all x1, waiting for transfers between devices, shards(): lax.all_to_all(rows, 'micro', split_axis=1, concat_axis=1, tiled=True)  12.3 us
  transfers between devices with their start and end apart: 29, of which 15 were waited for; matrix products, arithmetic and copies ran while one was open for 4% of the time, Pallas kernels for 0%

commit v1 on v0

--- a/solution.py
+++ b/solution.py
@@ -1,6 +1,8 @@
 import jax
 import jax.numpy as jnp
 from jax import lax
+from jax.experimental import pallas as pl
+from jax.experimental.pallas import tpu as pltpu
 from jax.sharding import PartitionSpec as P
 
 ITMAX = 4
@@ -11,9 +13,10 @@
 OMEGA = 0.8
 MASS = 0.1
 VOIGT = ((0, 5, 4), (5, 1, 3), (4, 3, 2))
-ALL_PAIRS = tuple(
-    ((first_axis, second_axis) for first_axis in range(6) for second_axis in range(6))
-)
+PAIRS = tuple((first, second) for first in range(6) for second in range(first, 6))
+PAIR_AT = {pair: at for at, pair in enumerate(PAIRS)}
+AROUND = tuple((dx, dy) for dx in (-1, 0, 1) for dy in (-1, 0, 1) if (dx, dy) != (0, 0))
+MESH = pl.DeviceIdType.MESH
 
 
 def with_halo(block, sides, width):
@@ -136,10 +139,9 @@
     wide = coupling.astype(jnp.float32)
     products = jnp.stack([wide[:, pair[0]] * wide[:, pair[1]] for pair in pairs], axis=1)
     extra = lax.dot_general(
-        products,
-        slope,
+        products.astype(jnp.bfloat16),
+        slope.astype(jnp.bfloat16),
         (((0,), (1,)), ((), ())),
-        precision=lax.Precision.HIGHEST,
         preferred_element_type=jnp.float32,
     )
     base = jnp.stack(
@@ -160,14 +162,314 @@
     return with_halo(field, (("macro", 1), ("micro", 2)), 1)
 
 
-def operate(field, tangent_ext):
-    strain = element_strain(extend(field))
-    stress = jnp.sum(tangent_ext * strain[None], axis=1)
-    return MASS * field + node_force(stress)[:, 1:-1, 1:-1, :-1]
-
-
-def two_products(residual, image):
-    return lax.psum((jnp.sum(residual * residual), jnp.sum(residual * image)), ("macro", "micro"))
+def cg_kernel(
+    sizes,
+    load_ref,
+    elem_ref,
+    inc_ref,
+    res_ref,
+    residual,
+    direction,
+    along,
+    increment,
+    image,
+    send_halo,
+    halo,
+    part,
+    got_micro,
+    middle,
+    got_macro,
+    send_sem,
+    recv_sem,
+    micro_send,
+    micro_recv,
+    macro_send,
+    macro_recv,
+):
+    count_x, count_y, n_macro, n_micro = sizes
+    wide = count_y + 2
+    rows, lanes = load_ref.shape[1], load_ref.shape[2]
+    a, b = lax.axis_index("macro"), lax.axis_index("micro")
+
+    def inside(dx, dy):
+        test = None
+        for place, step, count in ((a, dx, n_macro), (b, dy, n_micro)):
+            if step != 0:
+                good = (place > 0) if step < 0 else (place < count - 1)
+                test = good if test is None else jnp.logical_and(test, good)
+        return test
+
+    barrier = pltpu.get_barrier_semaphore()
+    for step in range(1, n_micro):
+        pl.semaphore_signal(
+            barrier, inc=1, device_id=(a, lax.rem(b + step, n_micro)), device_id_type=MESH
+        )
+    for step in range(1, n_macro):
+        pl.semaphore_signal(
+            barrier, inc=1, device_id=(lax.rem(a + step, n_macro), b), device_id_type=MESH
+        )
+    corners = [(dx, dy) for dx, dy in AROUND if dx != 0 and dy != 0]
+    for dx, dy in corners:
+        pl.semaphore_signal(
+            barrier,
+            inc=1,
+            device_id=(lax.rem(a + dx + n_macro, n_macro), lax.rem(b + dy + n_micro, n_micro)),
+            device_id_type=MESH,
+        )
+    pl.semaphore_wait(barrier, n_micro - 1 + n_macro - 1 + len(corners))
+    for at, (dx, dy) in enumerate(AROUND):
+
+        @pl.when(jnp.logical_not(inside(dx, dy)))
+        def _():
+            for it in range(ITERS + 1):
+                halo[it, at] = jnp.zeros(halo.shape[2:], jnp.float32)
+
+    def near(step, count):
+        return {0: list(range(1, count + 1)), -1: [1], 1: [count]}[step]
+
+    def far(step, count):
+        return {0: list(range(1, count + 1)), -1: [0], 1: [count + 1]}[step]
+
+    def places(at, pick):
+        dx, dy = AROUND[at]
+        return [i * wide + j for i in pick(dx, count_x) for j in pick(dy, count_y)]
+
+    def hop(it, at):
+        dx, dy = AROUND[at]
+        other = len(AROUND) - 1 - at
+        return pltpu.make_async_remote_copy(
+            src_ref=send_halo.at[it, at],
+            dst_ref=halo.at[it, other],
+            send_sem=send_sem.at[it, at],
+            recv_sem=recv_sem.at[it, other],
+            device_id=(a + dx, b + dy),
+            device_id_type=MESH,
+        )
+
+    def halo_start(it, ref):
+        for at, (dx, dy) in enumerate(AROUND):
+
+            @pl.when(inside(dx, dy))
+            def _():
+                mine = places(at, near)
+                for c in range(3):
+                    for k, row in enumerate(mine):
+                        send_halo[it, at, pl.ds(c * len(mine) + k, 1)] = ref[c, pl.ds(row, 1)]
+                hop(it, at).start()
+
+    def halo_finish(it, ref):
+        for at, (dx, dy) in enumerate(AROUND):
+
+            @pl.when(inside(dx, dy))
+            def _():
+                hop(it, at).wait_send()
+                pltpu.make_async_remote_copy(
+                    src_ref=send_halo.at[it, at],
+                    dst_ref=halo.at[it, at],
+                    send_sem=send_sem.at[it, at],
+                    recv_sem=recv_sem.at[it, at],
+                    device_id=(a + dx, b + dy),
+                    device_id_type=MESH,
+                ).wait_recv()
+
+        for at in range(len(AROUND)):
+            theirs = places(at, far)
+            for c in range(3):
+                for k, row in enumerate(theirs):
+                    ref[c, pl.ds(row, 1)] = halo[it, at, pl.ds(c * len(theirs) + k, 1)]
+
+    row_at = lax.broadcasted_iota(jnp.int32, (rows, lanes), 0)
+    lane_at = lax.broadcasted_iota(jnp.int32, (rows, lanes), 1)
+    own = row_at < 0
+    for i in range(1, count_x + 1):
+        low = i * wide + 1
+        own = jnp.logical_or(own, jnp.logical_and(row_at >= low, row_at < low + count_y))
+
+    def up(value, axis):
+        if axis == 2:
+            moved = pltpu.roll(value, lanes - 1, 1)
+            return jnp.where(lane_at == lanes - 1, 0.0, moved)
+        return pltpu.roll(value, rows - (wide if axis == 0 else 1), 0)
+
+    def down(value, axis):
+        if axis == 2:
+            return jnp.where(lane_at == 0, 0.0, pltpu.roll(value, 1, 1))
+        return pltpu.roll(value, wide if axis == 0 else 1, 0)
+
+    def strain_of(ref):
+        grads = []
+        for c in range(3):
+            value = ref[c]
+            moved = up(value, 2)
+            total, gap = value + moved, moved - value
+            total_up, gap_up = up(total, 1), up(gap, 1)
+            flat, slope_y, slope_z = total + total_up, total_up - total, gap + gap_up
+            grads.append(
+                (
+                    0.25 * (up(flat, 0) - flat),
+                    0.25 * (up(slope_y, 0) + slope_y),
+                    0.25 * (up(slope_z, 0) + slope_z),
+                )
+            )
+        return [
+            grads[0][0],
+            grads[1][1],
+            grads[2][2],
+            grads[1][2] + grads[2][1],
+            grads[0][2] + grads[2][0],
+            grads[0][1] + grads[1][0],
+        ]
+
+    def force_of(stress, c):
+        first, second, third = (stress[VOIGT[c][d]] for d in range(3))
+        first = first + down(first, 2)
+        second = second + down(second, 2)
+        third = down(third, 2) - third
+        first = first + down(first, 1)
+        rest = down(second, 1) - second + third + down(third, 1)
+        return 0.25 * (down(first, 0) - first + rest + down(rest, 0))
+
+    stress = [elem_ref[i] for i in range(6)]
+    for c in range(3):
+        residual[c] = jnp.where(own, load_ref[c] - force_of(stress, c), 0.0)
+        direction[c] = jnp.zeros((rows, lanes), jnp.float32)
+        along[c] = jnp.zeros((rows, lanes), jnp.float32)
+        increment[c] = jnp.zeros((rows, lanes), jnp.float32)
+    halo_start(ITERS, residual)
+    halo_finish(ITERS, residual)
+
+    def gather_start(it, src, dst, count, me, send, recv, device):
+        copies = []
+        for step in range(1, count):
+            copy = pltpu.make_async_remote_copy(
+                src_ref=src.at[it],
+                dst_ref=dst.at[it, me],
+                send_sem=send.at[it, step - 1],
+                recv_sem=recv.at[it, step - 1],
+                device_id=device(lax.rem(me + step, count)),
+                device_id_type=MESH,
+            )
+            copy.start()
+            copies.append(copy)
+        dst[it, me] = src[it]
+        return copies
+
+    def gather_finish(it, copies, dst, count):
+        for copy in copies:
+            copy.wait()
+        total = dst[it, 0]
+        for at in range(1, count):
+            total = total + dst[it, at]
+        return total
+
+    def step_body(it, carry):
+        norm_old, alpha_old = carry
+        strain = strain_of(residual)
+        stress = []
+        for i in range(6):
+            value = None
+            for j in range(6):
+                term = elem_ref[6 + PAIR_AT[(min(i, j), max(i, j))]] * strain[j]
+                value = term if value is None else value + term
+            stress.append(value)
+        norm = jnp.zeros((rows, lanes), jnp.float32)
+        cross = jnp.zeros((rows, lanes), jnp.float32)
+        for c in range(3):
+            here = residual[c]
+            new = jnp.where(own, MASS * here + force_of(stress, c), 0.0)
+            image[c] = new
+            kept = jnp.where(own, here, 0.0)
+            norm = norm + kept * kept
+            cross = cross + kept * new
+
+        def folded(value):
+            value = jnp.sum(value, axis=0, keepdims=True)
+            total = value[:, :128]
+            for at in range(128, lanes, 128):
+                total = total + value[:, at : at + 128]
+            return total
+
+        tile_row = lax.broadcasted_iota(jnp.int32, (8, 128), 0)
+        part[it] = jnp.where(
+            tile_row == 0, folded(norm), jnp.where(tile_row == 1, folded(cross), 0.0)
+        )
+        copies = gather_start(
+            it, part, got_micro, n_micro, b, micro_send, micro_recv, lambda other: (a, other)
+        )
+        halo_start(it, image)
+        middle[it] = gather_finish(it, copies, got_micro, n_micro)
+        copies = gather_start(
+            it, middle, got_macro, n_macro, a, macro_send, macro_recv, lambda other: (other, b)
+        )
+        halo_finish(it, image)
+        totals = jnp.sum(gather_finish(it, copies, got_macro, n_macro), axis=1, keepdims=True)
+        norm_now, product = totals[0:1], totals[1:2]
+        first = jnp.full((1, 1), it, jnp.int32) == 0
+        ratio = jnp.where(first, 0.0, norm_now / norm_old)
+        alpha = norm_now / (product - ratio * norm_now / alpha_old)
+        for c in range(3):
+            here = residual[c]
+            toward = here + ratio * direction[c]
+            drop = image[c] + ratio * along[c]
+            direction[c] = toward
+            along[c] = drop
+            increment[c] = increment[c] + alpha * toward
+            residual[c] = here - alpha * drop
+        return norm_now, alpha
+
+    lax.fori_loop(
+        0, ITERS, step_body, (jnp.ones((1, 1), jnp.float32), jnp.ones((1, 1), jnp.float32))
+    )
+    for c in range(3):
+        for i in range(count_x):
+            low = (i + 1) * wide + 1
+            inc_ref[c, i] = increment[c, pl.ds(low, count_y)]
+            res_ref[c, i] = residual[c, pl.ds(low, count_y)]
+
+
+def conjugate_gradients(load, elements):
+    _, count_x, count_y, count_z = load.shape
+    n_macro, n_micro = lax.axis_size("macro"), lax.axis_size("micro")
+    flat = (count_x + 2) * (count_y + 2)
+    rows = -(-flat // 8) * 8
+
+    def laid(value, high):
+        value = jnp.pad(value, ((0, 0), (1 - high, 1), (1 - high, 1), (0, 0)))
+        value = value.reshape(value.shape[0], flat, count_z)
+        return jnp.pad(value, ((0, 0), (0, rows - flat), (0, 0)))
+
+    side = -(-3 * max(count_x, count_y) // 8) * 8
+    node = pltpu.VMEM((3, rows, count_z), jnp.float32)
+    around = pltpu.VMEM((ITERS + 1, len(AROUND), side, count_z), jnp.float32)
+    dma = pltpu.SemaphoreType.DMA
+
+    def body(*refs):
+        cg_kernel((count_x, count_y, n_macro, n_micro), *refs)
+
+    vmem = pl.BlockSpec(memory_space=pltpu.VMEM)
+    return pl.pallas_call(
+        body,
+        out_shape=[jax.ShapeDtypeStruct(load.shape, jnp.float32)] * 2,
+        in_specs=[vmem, vmem],
+        out_specs=[vmem, vmem],
+        scratch_shapes=[node] * 5
+        + [
+            around,
+            around,
+            pltpu.VMEM((ITERS, 8, 128), jnp.float32),
+            pltpu.VMEM((ITERS, n_micro, 8, 128), jnp.float32),
+            pltpu.VMEM((ITERS, 8, 128), jnp.float32),
+            pltpu.VMEM((ITERS, n_macro, 8, 128), jnp.float32),
+            dma((ITERS + 1, len(AROUND))),
+            dma((ITERS + 1, len(AROUND))),
+            dma((ITERS, n_micro - 1)),
+            dma((ITERS, n_micro - 1)),
+            dma((ITERS, n_macro - 1)),
+            dma((ITERS, n_macro - 1)),
+        ],
+        compiler_params=pltpu.CompilerParams(collective_id=0, has_side_effects=True),
+        name="conjugate_gradients",
+    )(laid(load, 0), laid(elements, 1))
 
 
 def shards(
@@ -197,12 +499,12 @@
     onehot = (owner_of[:, None] == jnp.arange(owners, dtype=jnp.int32)[None, :]).astype(jnp.int32)
     ranks = jnp.sum((jnp.cumsum(onehot, axis=0) - 1) * onehot, axis=1)
     target = owner_of * capacity + ranks
-    send_strain = jnp.zeros((6, owners * capacity), jnp.float32).at[:, target].set(strain_points)
-    send_sweeps = jnp.zeros((1, owners * capacity), jnp.int32).at[0, target].set(sweeps_of)
-    got_strain, got_sweeps = (
-        lax.all_to_all(send_strain, "micro", split_axis=1, concat_axis=1, tiled=True),
-        lax.all_to_all(send_sweeps, "micro", split_axis=1, concat_axis=1, tiled=True),
-    )
+    bundle = jnp.concatenate([strain_points, sweeps_of.astype(jnp.float32)[None]], axis=0)
+    send = jnp.zeros((7, owners * capacity), jnp.float32).at[:, target].set(
+        bundle, unique_indices=True, mode="promise_in_bounds"
+    )
+    got = lax.all_to_all(send, "micro", split_axis=1, concat_axis=1, tiled=True)
+    got_strain, got_sweeps = got[:6], got[6:]
     rows = micro_solve(
         got_strain,
         got_sweeps,
@@ -212,40 +514,16 @@
         coupling[0],
         lame_first[0],
         lame_shear[0],
-        ALL_PAIRS,
+        PAIRS,
     )
     back = lax.all_to_all(rows, "micro", split_axis=1, concat_axis=1, tiled=True)
-    values = jnp.take(back, target, axis=1)
-    values = values.reshape(42, count_x, count_y, count_z)
+    values = jnp.take(back, target, axis=1, unique_indices=True, mode="clip")
+    values = values.reshape(back.shape[0], count_x, count_y, count_z)
     left_x = passed_along(values[:, -1:], "macro", 1)
     values = jnp.concatenate([left_x, values], axis=1)
     left_y = passed_along(values[:, :, -1:], "micro", 1)
     values = jnp.concatenate([left_y, values], axis=2)
-    stress_ext = values[:6]
-    tangent_ext = values[6:].reshape(6, 6, count_x + 1, count_y + 1, count_z)
-    rhs = load - node_force(stress_ext)[:, 1:-1, 1:-1, :-1]
-
-    def apply(field):
-        return operate(field, tangent_ext)
-
-    increment = jnp.zeros_like(rhs)
-    residual = rhs
-    image = apply(residual)
-    norm_now, product = two_products(residual, image)
-    alpha = norm_now / product
-    direction, along = (residual, image)
-    for step in range(ITERS):
-        increment = increment + alpha * direction
-        residual = residual - alpha * along
-        if step + 1 < ITERS:
-            image = apply(residual)
-            norm_next, product = two_products(residual, image)
-            ratio = norm_next / norm_now
-            alpha = norm_next / (product - ratio * norm_next / alpha)
-            direction = residual + ratio * direction
-            along = image + ratio * along
-            norm_now = norm_next
-    return (increment, residual)
+    return tuple(conjugate_gradients(load, values))
 
 
 def solution(mesh):

time: 449 us -> 161 us (0.36)
  blocking collectives: 212 us -> 0 us
  Pallas kernels: 0 us -> 49.6 us
  starting transfers between devices: 71.2 us -> 24.1 us
  waiting for transfers between devices: 59.1 us -> 18.8 us
  between operations: 20.8 us -> 2.3 us
  other arithmetic: 19.8 us -> 7.06 us
    psum x5 -> x0, blocking collectives: 212 us -> none  [two_products(): lax.psum((jnp.sum(residual * residual), jnp.sum(residual * image)), ('mac...]
    pallas_call x0 -> x1, Pallas kernels: none -> 49.6 us  [conjugate_gradients(): pl.pallas_call(body, out_shape=[jax.ShapeDtypeStruct(load.shape, jnp.floa...]
    ppermute x12 -> x2, waiting for transfers between devices: 38.2 us -> 2.72 us  [with_halo(): lax.ppermute(lax.slice_in_dim(block, 0, width, axis=dim), axis, backward)]
    ppermute x12 -> x2, starting transfers between devices: 35.5 us -> 6.32 us  [with_halo(): lax.ppermute(lax.slice_in_dim(block, block.shape[dim] - width, None, axis...]
    ppermute x12 -> x2, starting transfers between devices: 15.5 us -> 2.58 us  [with_halo(): lax.ppermute(lax.slice_in_dim(block, 0, width, axis=dim), axis, backward)]
    all_to_all x2 -> x1, starting transfers between devices: 10.6 us -> 5.91 us  [shards(): got = lax.all_to_all(send, 'micro', split_axis=1, concat_axis=1, tiled=True)]
  transfers between devices with their start and end apart: 29 -> 8, of which waited for: 15 -> 5; matrix products, arithmetic and copies ran while one was open for 4% -> 5% of each run, Pallas kernels for 0% -> 0%
where the time goes in v1:
time: 161 us; the launch traced here: 160 us
  Pallas kernels  49.6 us (31%)
  matrix products  42.5 us (26%)
  starting transfers between devices  24.1 us (15%)
  waiting for transfers between devices  18.8 us (12%)
  local copies, waits for them, and re-layouts  15.6 us (10%)
  other arithmetic  7.06 us (4%)
  between operations  2.3 us (1%)
    pallas_call x1, Pallas kernels, conjugate_gradients(): pl.pallas_call(body, out_shape=[jax.ShapeDtypeStruct(load.shape, jnp.floa...  49.6 us
    dot_general x4, matrix products, micro_solve(): jnp.dot(misfit.astype(jnp.bfloat16), precond, preferred_element_type=jnp....  36.1 us
    all_to_all x1, waiting for transfers between devices, shards(): lax.all_to_all(rows, 'micro', split_axis=1, concat_axis=1, tiled=True)  9.62 us
    ppermute x2, starting transfers between devices, with_halo(): lax.ppermute(lax.slice_in_dim(block, block.shape[dim] - width, None, axis...  6.32 us
    all_to_all x1, starting transfers between devices, shards(): got = lax.all_to_all(send, 'micro', split_axis=1, concat_axis=1, tiled=True)  5.91 us
    ppermute x2, starting transfers between devices, passed_along(): lax.ppermute(value, axis, [(source, source + steps) for source in range(i...  5.83 us
    all_to_all x1, waiting for transfers between devices, shards(): got = lax.all_to_all(send, 'micro', split_axis=1, concat_axis=1, tiled=True)  4.38 us
    unnamed x20, local copies, waits for them, and re-layouts  3.93 us
  transfers between devices with their start and end apart: 8, of which 5 were waited for; matrix products, arithmetic and copies ran while one was open for 5% of the time, Pallas kernels for 0%

profile of v1, /device:TPU:0, one launch (start us, length us, event | category | flops | bytes accessed | tf_op | source)
XLA Modules:
  0.0 159.8 jit_solution(3390195343741063288)
XLA Ops:
  0.7 0.8 fusion.50
  1.4 4.9 %collective-permute-start = (f32[3,1,2,256]{3,2,1,0:T(2,128)S(1)}, f32[3,1,2,256]{3,2,1,0:T(2,128)S(1)}, u32[]{:S(2)}, u32[]{:S(2)}) collective-permute-start(f32[3,1,2,256]{3,2,1,0:T(2,128)S(1)} %get-tuple-element.41), channel_id=1, source_target_pairs={{0,8},{8,16},{16,24},{1,9},{9,17},{17,25},{2,10},{10,18},{18,26},{... | collective-permute-start | bytes 18440 | tf_op jit(solution)/shard_map/ppermute | solution.py:27
  6.3 1.3 collective-permute-start.1
  8.3 2.3 %reduce-window.6 = s32[8,8,128]{2,1,0:T(8,128)S(1)} reduce-window(s32[8,8,128]{2,1,0:T(8,128)S(1)} %fusion.39, s32[]{:T(128)} %constant.15.clone.1), window={size=1x1x128 pad=0_0x0_0x127_0}, to_apply=%region_0.1 | reduce-window | flops 1040384 | bytes 65540 | tf_op jit(solution)/shard_map/reduce-window
  11.1 0.7 bitcast_convert_fusion
  11.8 0.7 fusion.38
  12.5 0.7 compare_select_fusion
  13.2 0.7 constant_dynamic-update-slice_fusion.1
  14.0 1.5 collective-permute-start.2
  15.5 1.3 collective-permute-start.3
  17.5 2.7 %collective-permute-done.3 = f32[3,4,1,256]{3,2,1,0:T(1,128)S(1)} collective-permute-done((f32[3,4,1,256]{3,2,1,0:T(1,128)S(1)}, f32[3,4,1,256]{3,2,1,0:T(1,128)S(1)}, u32[]{:S(2)}, u32[]{:S(2)}) %collective-permute-start.3) | collective-permute-done | bytes 12320 | tf_op jit(solution)/shard_map/ppermute | solution.py:30
  21.1 3.3 %scatter_custom_fusion = f32[7,2048]{0,1:T(8,128)S(1)} fusion(s32[1024]{0:T(1024)S(1)} %bitcast.108, f32[1024,7]{1,0:T(8,128)S(1)} %copy.29, f32[]{:T(128)} %constant.13.clone.1), kind=kCustom, calls=%fused_computation.27 | custom fusion | bytes 57348 | tf_op jit(solution)/shard_map/scatter | solution.py:503
  24.4 0.9 copy.30
  25.4 5.9 %all-to-all-start = ((f32[7,8,256]{2,0,1:T(8,128)}), f32[7,8,256]{2,0,1:T(8,128)S(1)}, u32[]{:S(2)}, u32[]{:S(2)}) async-start(f32[7,8,256]{2,0,1:T(8,128)} %copy.30), calls=%async_computation | async-start | bytes 131072 | tf_op jit(solution)/shard_map/all_to_all | solution.py:506
  32.8 4.4 %all-to-all-done = f32[7,8,256]{2,0,1:T(8,128)S(1)} async-done(((f32[7,8,256]{2,0,1:T(8,128)}), f32[7,8,256]{2,0,1:T(8,128)S(1)}, u32[]{:S(2)}, u32[]{:S(2)}) %all-to-all-start) | async-done | bytes 57376 | tf_op jit(solution)/shard_map/all_to_all | solution.py:506
  37.4 2.7 %fusion.41 = f32[2048,512]{1,0:T(8,128)} fusion(bf16[6,2048]{1,0:T(8,128)(2,1)S(1)} %bitcast.96, bf16[1,6,512]{2,1,0:T(8,128)(2,1)S(1)} %copy-done.4), kind=kOutput, calls=%fused_computation.91 | convolution fusion | flops 12582912 | bytes 4225024 | tf_op jit(solution)/shard_map/dot_general | solution.py:107
  40.1 6.6 %subtract_select_fusion.3 = f32[2048,512]{1,0:T(8,128)} fusion(pred[2048]{0:T(1024)(128)(4,1)S(1)} %gt.63, f32[2048,512]{1,0:T(8,128)} %fusion.41, bf16[1,512,512]{2,1,0:T(8,128)(2,1)S(1)} %copy-done, bf16[1,512,512]{2,1,0:T(8,128)(2,1)S(1)} %copy-done.5), kind=kOutput, calls=%fused_computation.9 | convolution fusion | flops 2152726528 | bytes 9439232 | tf_op jit(solution)/shard_map/dot_general | solution.py:117
  46.6 9.7 %subtract_select_fusion.2 = f32[2048,512]{1,0:T(8,128)} fusion(f32[2048,512]{1,0:T(8,128)} %subtract_select_fusion.3, pred[2048]{0:T(1024)(128)(4,1)S(1)} %gt.60, f32[2048,512]{1,0:T(8,128)} %fusion.41, bf16[1,512,512]{2,1,0:T(8,128)(2,1)S(1)} %copy-done, bf16[1,512,512]{2,1,0:T(8,128)(2,1)S(1)} %copy-done.5), kind=kOutput, calls=%fused_computation.4 | convolution fusion | flops 2155872256 | bytes 13633536 | tf_op jit(solution)/shard_map/dot_general | solution.py:117
  56.4 10.1 %subtract_select_fusion.1 = f32[2048,512]{1,0:T(8,128)} fusion(f32[2048,512]{1,0:T(8,128)} %subtract_select_fusion.2, pred[2048]{0:T(1024)(128)(4,1)S(1)} %gt.57, f32[2048,512]{1,0:T(8,128)} %fusion.41, bf16[1,512,512]{2,1,0:T(8,128)(2,1)S(1)} %copy-done, bf16[1,512,512]{2,1,0:T(8,128)(2,1)S(1)} %copy-done.5), kind=kOutput, calls=%fused_computation.3 | convolution fusion | flops 2155872256 | bytes 13633536 | tf_op jit(solution)/shard_map/dot_general | solution.py:117
  66.5 9.7 %subtract_select_fusion = f32[2048,512]{1,0:T(8,128)} fusion(f32[2048,512]{1,0:T(8,128)} %subtract_select_fusion.1, pred[2048]{0:T(1024)(128)(4,1)S(1)} %gt.54, f32[2048,512]{1,0:T(8,128)} %fusion.41, bf16[1,512,512]{2,1,0:T(8,128)(2,1)S(1)} %copy-done, bf16[1,512,512]{2,1,0:T(8,128)(2,1)S(1)} %copy-done.5), kind=kOutput, calls=%fused_computation.2 | convolution fusion | flops 2155872256 | bytes 13633536 | tf_op jit(solution)/shard_map/dot_general | solution.py:117
  76.4 3.0 %fusion = f32[6,2048]{1,0:T(8,128)S(1)} fusion(f32[6,2048]{1,0:T(8,128)S(1)} %stack.18, f32[2048,512]{1,0:T(8,128)} %subtract_select_fusion, bf16[1,512,6]{1,2,0:T(8,128)(2,1)S(1)} %copy-done.2), kind=kOutput, calls=%fused_computation.13 | convolution fusion | flops 13643776 | bytes 4298752 | tf_op jit(solution)/shard_map/dot_general | solution.py:132
  80.6 0.8 copy.31
  81.4 3.4 %all-to-all-start.1 = ((f32[27,8,256]{2,0,1:T(8,128)}), f32[27,8,256]{2,0,1:T(8,128)S(1)}, u32[]{:S(2)}, u32[]{:S(2)}) async-start(f32[27,8,256]{2,0,1:T(8,128)} %copy.31), calls=%async_computation.1 | async-start | bytes 524288 | tf_op jit(solution)/shard_map/all_to_all | solution.py:519
  84.8 9.6 %all-to-all-done.1 = f32[27,8,256]{2,0,1:T(8,128)S(1)} async-done(((f32[27,8,256]{2,0,1:T(8,128)}), f32[27,8,256]{2,0,1:T(8,128)S(1)}, u32[]{:S(2)}, u32[]{:S(2)}) %all-to-all-start.1) | async-done | bytes 221216 | tf_op jit(solution)/shard_map/all_to_all | solution.py:519
  94.8 2.8 %gather_fusion = f32[1024,27]{1,0:T(8,128)S(1)} fusion(f32[27,2048]{0,1:T(8,128)S(1)} %bitcast.91, s32[1024]{0:T(1024)S(1)} %broadcast_clamp_fusion), kind=kCustom, calls=%fused_computation | custom fusion | bytes 225280 | tf_op jit(solution)/shard_map/jit(_take)/gather | solution.py:520
  97.9 4.5 %collective-permute-start.4 = (f32[27,1,2,256]{3,2,1,0:T(2,128)S(1)}, f32[27,1,2,256]{3,2,1,0:T(2,128)S(1)}, u32[]{:S(2)}, u32[]{:S(2)}) collective-permute-start(f32[27,1,2,256]{3,2,1,0:T(2,128)S(1)} %slice.259), channel_id=1, source_target_pairs={{0,8},{8,16},{16,24},{1,9},{9,17},{17,25},{2,10},{10,18},{18,26},{... | collective-permute-start | bytes 165896 | tf_op jit(solution)/shard_map/ppermute | solution.py:38
  102.4 1.8 %collective-permute-done.4 = f32[27,1,2,256]{3,2,1,0:T(2,128)S(1)} collective-permute-done((f32[27,1,2,256]{3,2,1,0:T(2,128)S(1)}, f32[27,1,2,256]{3,2,1,0:T(2,128)S(1)}, u32[]{:S(2)}, u32[]{:S(2)}) %collective-permute-start.4) | collective-permute-done | bytes 55328 | tf_op jit(solution)/shard_map/ppermute | solution.py:38
  104.3 1.3 collective-permute-start.5
  106.7 0.9 reshape.261.refs_1_
  107.7 49.6 %conjugate_gradients.1 = (f32[3,2,2,256]{3,2,1,0:T(2,128)}, f32[3,2,2,256]{3,2,1,0:T(2,128)}) custom-call(f32[3,16,256]{2,1,0:T(8,128)} %reshape.257.refs_0_, f32[27,16,256]{2,1,0:T(8,128)} %reshape.261.refs_1_), custom_call_target="tpu_custom_call" | custom-call | tf_op jit(solution)/shard_map/conjugate_gradients/pallas_call | solution.py:450
  157.2 1.3 copy.49
  158.5 1.3 copy.50
  (63 shorter events, 6.4 us)
Async XLA Ops:
  0.6 39.4 %copy-start = (bf16[1,512,512]{2,1,0:T(8,128)(2,1)S(1)}, bf16[1,512,512]{2,1,0:T(8,128)(2,1)}, u32[]{:S(2)}) copy-start(bf16[1,512,512]{2,1,0:T(8,128)(2,1)} %param.15) | copy-start | bytes 1572868
  0.6 36.7 %copy-start.4 = (bf16[1,6,512]{2,1,0:T(8,128)(2,1)S(1)}, bf16[1,6,512]{2,1,0:T(8,128)(2,1)}, u32[]{:S(2)}) copy-start(bf16[1,6,512]{2,1,0:T(8,128)(2,1)} %param.16) | copy-start | bytes 18436
  1.4 11.8 %collective-permute-start = (f32[3,1,2,256]{3,2,1,0:T(2,128)S(1)}, f32[3,1,2,256]{3,2,1,0:T(2,128)S(1)}, u32[]{:S(2)}, u32[]{:S(2)}) collective-permute-start(f32[3,1,2,256]{3,2,1,0:T(2,128)S(1)} %get-tuple-element.41), channel_id=1, source_target_pairs={{0,8},{8,16},{16,24},{1,9},{9,17},{17,25},{2,10},{10,18},{18,26},{... | collective-permute-start | bytes 18440 | tf_op jit(solution)/shard_map/ppermute | solution.py:27
  6.3 7.7 %collective-permute-start.1 = (f32[3,1,2,256]{3,2,1,0:T(2,128)S(1)}, f32[3,1,2,256]{3,2,1,0:T(2,128)S(1)}, u32[]{:S(2)}, u32[]{:S(2)}) collective-permute-start(f32[3,1,2,256]{3,2,1,0:T(2,128)S(1)} %get-tuple-element.40), channel_id=1, source_target_pairs={{8,0},{16,8},{24,16},{9,1},{17,9},{25,17},{10,2},{18,10},{26,18},{... | collective-permute-start | bytes 18440 | tf_op jit(solution)/shard_map/ppermute | solution.py:30
  14.0 3.5 %collective-permute-start.2 = (f32[3,4,1,256]{3,2,1,0:T(1,128)S(1)}, f32[3,4,1,256]{3,2,1,0:T(1,128)S(1)}, u32[]{:S(2)}, u32[]{:S(2)}) collective-permute-start(f32[3,4,1,256]{3,2,1,0:T(1,128)S(1)} %get-tuple-element.17), channel_id=1, source_target_pairs={{0,1},{1,2},{2,3},{3,4},{4,5},{5,6},{6,7},{8,9},{9,10},{10,11},{11... | collective-permute-start | bytes 36872 | tf_op jit(solution)/shard_map/ppermute | solution.py:27
  15.5 4.7 %collective-permute-start.3 = (f32[3,4,1,256]{3,2,1,0:T(1,128)S(1)}, f32[3,4,1,256]{3,2,1,0:T(1,128)S(1)}, u32[]{:S(2)}, u32[]{:S(2)}) collective-permute-start(f32[3,4,1,256]{3,2,1,0:T(1,128)S(1)} %get-tuple-element.18), channel_id=1, source_target_pairs={{1,0},{2,1},{3,2},{4,3},{5,4},{6,5},{7,6},{9,8},{10,9},{11,10},{12... | collective-permute-start | bytes 36872 | tf_op jit(solution)/shard_map/ppermute | solution.py:30
  20.2 19.9 %copy-start.5 = (bf16[1,512,512]{2,1,0:T(8,128)(2,1)S(1)}, bf16[1,512,512]{2,1,0:T(8,128)(2,1)}, u32[]{:S(2)}) copy-start(bf16[1,512,512]{2,1,0:T(8,128)(2,1)} %param.14) | copy-start | bytes 1572868
  25.4 11.8 %all-to-all-start = ((f32[7,8,256]{2,0,1:T(8,128)}), f32[7,8,256]{2,0,1:T(8,128)S(1)}, u32[]{:S(2)}, u32[]{:S(2)}) async-start(f32[7,8,256]{2,0,1:T(8,128)} %copy.30), calls=%async_computation | async-start | bytes 131072 | tf_op jit(solution)/shard_map/all_to_all | solution.py:506
  66.5 9.9 %copy-start.2 = (bf16[1,512,6]{1,2,0:T(8,128)(2,1)S(1)}, bf16[1,512,6]{1,2,0:T(8,128)(2,1)}, u32[]{:S(2)}) copy-start(bf16[1,512,6]{1,2,0:T(8,128)(2,1)} %param.17) | copy-start | bytes 18436
  76.4 3.5 %copy-start.1 = (f32[2048,512]{1,0:T(8,128)S(1)}, f32[2048,512]{1,0:T(8,128)}, u32[]{:S(2)}) copy-start(f32[2048,512]{1,0:T(8,128)} %subtract_select_fusion) | copy-start | bytes 12582916
  79.8 25.8 %copy-start.3 = (f32[3,2,2,256]{3,2,1,0:T(2,128)S(1)}, f32[3,2,2,256]{3,2,1,0:T(2,128)}, u32[]{:S(2)}) copy-start(f32[3,2,2,256]{3,2,1,0:T(2,128)} %param.11) | copy-start | bytes 36868
  81.4 13.1 %all-to-all-start.1 = ((f32[27,8,256]{2,0,1:T(8,128)}), f32[27,8,256]{2,0,1:T(8,128)S(1)}, u32[]{:S(2)}, u32[]{:S(2)}) async-start(f32[27,8,256]{2,0,1:T(8,128)} %copy.31), calls=%async_computation.1 | async-start | bytes 524288 | tf_op jit(solution)/shard_map/all_to_all | solution.py:519
  97.9 6.3 %collective-permute-start.4 = (f32[27,1,2,256]{3,2,1,0:T(2,128)S(1)}, f32[27,1,2,256]{3,2,1,0:T(2,128)S(1)}, u32[]{:S(2)}, u32[]{:S(2)}) collective-permute-start(f32[27,1,2,256]{3,2,1,0:T(2,128)S(1)} %slice.259), channel_id=1, source_target_pairs={{0,8},{8,16},{16,24},{1,9},{9,17},{17,25},{2,10},{10,18},{18,26},{... | collective-permute-start | bytes 165896 | tf_op jit(solution)/shard_map/ppermute | solution.py:38
  104.3 2.2 %collective-permute-start.5 = (f32[27,3,1,256]{3,2,1,0:T(1,128)S(1)}, f32[27,3,1,256]{3,2,1,0:T(1,128)S(1)}, u32[]{:S(2)}, u32[]{:S(2)}) collective-permute-start(f32[27,3,1,256]{3,2,1,0:T(1,128)S(1)} %pad_maximum_fusion.1), channel_id=1, source_target_pairs={{0,1},{1,2},{2,3},{3,4},{4,5},{5,6},{6,7},{8,9},{9,10},{10,11},{11... | collective-permute-start | bytes 248840 | tf_op jit(solution)/shard_map/ppermute | solution.py:38

commit v2 on v1

--- a/solution.py
+++ b/solution.py
@@ -100,62 +100,88 @@
     return forces
 
 
-def micro_solve(
-    strain, sweeps, stiffness, precond, forcing, coupling, lame_first, lame_shear, pairs
-):
-    strain_half = strain.astype(jnp.bfloat16)
-    modal_load = lax.dot_general(
-        strain_half, forcing, (((0,), (0,)), ((), ())), preferred_element_type=jnp.float32
-    )
-    modes = jnp.zeros_like(modal_load)
+def micro_kernel(bundle_ref, stiff_ref, pre_ref, force_ref, couple_ref, product_ref, coef_ref, out_ref):
+    bundle = bundle_ref[...]
+    sweeps = bundle[6:7]
+    modal_load = jnp.dot(
+        force_ref[...], bundle.astype(jnp.bfloat16), preferred_element_type=jnp.float32
+    )
+    modes = None
     for sweep in range(ITMAX):
-        misfit = (
-            jnp.dot(modes.astype(jnp.bfloat16), stiffness, preferred_element_type=jnp.float32)
-            + BETA * jnp.tanh(modes)
-            - modal_load
-        )
-        update = modes - OMEGA * jnp.dot(
-            misfit.astype(jnp.bfloat16), precond, preferred_element_type=jnp.float32
-        )
-        modes = jnp.where((sweeps[0] > sweep)[:, None], update, modes)
-    trace = strain[0] + strain[1] + strain[2]
-    elastic = jnp.stack(
-        [
-            lame_first * trace + 2.0 * lame_shear * strain[0],
-            lame_first * trace + 2.0 * lame_shear * strain[1],
-            lame_first * trace + 2.0 * lame_shear * strain[2],
-            lame_shear * strain[3],
-            lame_shear * strain[4],
-            lame_shear * strain[5],
-        ]
-    )
-    stress = elastic + lax.dot_general(
-        coupling,
-        modes.astype(jnp.bfloat16),
-        (((0,), (1,)), ((), ())),
-        preferred_element_type=jnp.float32,
-    )
-    slope = 1.0 - jnp.tanh(modes) ** 2
-    wide = coupling.astype(jnp.float32)
-    products = jnp.stack([wide[:, pair[0]] * wide[:, pair[1]] for pair in pairs], axis=1)
-    extra = lax.dot_general(
-        products.astype(jnp.bfloat16),
-        slope.astype(jnp.bfloat16),
-        (((0,), (1,)), ((), ())),
-        preferred_element_type=jnp.float32,
-    )
-    base = jnp.stack(
-        [
-            lame_first * float(pair[0] < 3 and pair[1] < 3)
-            + lame_shear
-            * (
-                2.0 * float(pair[0] == pair[1] and pair[0] < 3)
-                + float(pair[0] == pair[1] and pair[0] >= 3)
+        misfit = -modal_load
+        if modes is not None:
+            misfit = (
+                jnp.dot(
+                    stiff_ref[...], modes.astype(jnp.bfloat16), preferred_element_type=jnp.float32
+                )
+                + BETA * jnp.tanh(modes)
+                - modal_load
             )
-            for pair in pairs
-        ]
-    )
-    return jnp.concatenate([stress, extra + base[:, None]], axis=0)
+        change = OMEGA * jnp.dot(
+            pre_ref[...], misfit.astype(jnp.bfloat16), preferred_element_type=jnp.float32
+        )
+        before = jnp.zeros_like(change) if modes is None else modes
+        modes = jnp.where(sweeps > sweep, before - change, before)
+    bent = jnp.tanh(modes)
+    slope = 1.0 - bent * bent
+    trace = bundle[0:1] + bundle[1:2] + bundle[2:3]
+    rows = coef_ref.shape[0]
+    tall = jnp.concatenate(
+        [bundle, jnp.zeros((rows - bundle.shape[0], bundle.shape[1]), jnp.float32)], axis=0
+    )
+    coef = coef_ref[...]
+    total = coef[:, 0:1] * trace + coef[:, 1:2] * tall + coef[:, 2:3]
+    total = total + jnp.dot(
+        couple_ref[...], modes.astype(jnp.bfloat16), preferred_element_type=jnp.float32
+    )
+    total = total + jnp.dot(
+        product_ref[...], slope.astype(jnp.bfloat16), preferred_element_type=jnp.float32
+    )
+    out_ref[...] = total[: out_ref.shape[0]]
+
+
+def micro_solve(bundle, stiffness, precond, forcing, coupling, lame_first, lame_shear, pairs):
+    size, points = stiffness.shape[0], bundle.shape[1]
+    tile = 512 if points % 512 == 0 else points
+    count = 6 + len(pairs)
+    rows = -(-count // 8) * 8
+    force = jnp.pad(forcing.T, ((0, 0), (0, 2)))
+    wide = coupling.astype(jnp.float32).T
+    products = jnp.stack([wide[first] * wide[second] for first, second in pairs])
+    products = jnp.pad(products.astype(jnp.bfloat16), ((6, rows - count), (0, 0)))
+    couple = jnp.pad(coupling.T, ((0, rows - 6), (0, 0)))
+    on_trace = jnp.array([1.0] * 3 + [0.0] * (rows - 3), jnp.float32)
+    on_shear = jnp.array([2.0] * 3 + [1.0] * 3 + [0.0] * (rows - 6), jnp.float32)
+    base_first = [0.0] * 6 + [float(i < 3 and j < 3) for i, j in pairs] + [0.0] * (rows - count)
+    base_shear = (
+        [0.0] * 6
+        + [float(i == j) * (2.0 if i < 3 else 1.0) for i, j in pairs]
+        + [0.0] * (rows - count)
+    )
+    base = lame_first * jnp.array(base_first, jnp.float32) + lame_shear * jnp.array(
+        base_shear, jnp.float32
+    )
+    coef = jnp.stack([lame_first * on_trace, lame_shear * on_shear, base], axis=1)
+
+    def whole(shape):
+        return pl.BlockSpec(shape, lambda i: (0, 0))
+
+    return pl.pallas_call(
+        micro_kernel,
+        grid=(points // tile,),
+        out_shape=jax.ShapeDtypeStruct((count, points), jnp.float32),
+        in_specs=[
+            pl.BlockSpec((8, tile), lambda i: (0, i)),
+            whole((size, size)),
+            whole((size, size)),
+            whole((size, 8)),
+            whole((rows, size)),
+            whole((rows, size)),
+            whole((rows, 3)),
+        ],
+        out_specs=pl.BlockSpec((count, tile), lambda i: (0, i)),
+        name="micro_solve",
+    )(bundle, stiffness, precond, force, couple, products, coef)
 
 
 def extend(field):
@@ -500,14 +526,13 @@
     ranks = jnp.sum((jnp.cumsum(onehot, axis=0) - 1) * onehot, axis=1)
     target = owner_of * capacity + ranks
     bundle = jnp.concatenate([strain_points, sweeps_of.astype(jnp.float32)[None]], axis=0)
-    send = jnp.zeros((7, owners * capacity), jnp.float32).at[:, target].set(
+    bundle = jnp.pad(bundle, ((0, 1), (0, 0)))
+    send = jnp.zeros((8, owners * capacity), jnp.float32).at[:, target].set(
         bundle, unique_indices=True, mode="promise_in_bounds"
     )
     got = lax.all_to_all(send, "micro", split_axis=1, concat_axis=1, tiled=True)
-    got_strain, got_sweeps = got[:6], got[6:]
     rows = micro_solve(
-        got_strain,
-        got_sweeps,
+        got,
         stiffness[0],
         precond[0],
         forcing[0],

time: 161 us -> 131 us (0.81)
  matrix products: 42.5 us -> 0 us
  Pallas kernels: 49.6 us -> 63.6 us
  other arithmetic: 7.06 us -> 3.46 us
  local copies, waits for them, and re-layouts: 15.6 us -> 19.1 us
    dot_general x7 -> x0, matrix products: 42.5 us -> none  [the longest x4 36.1 us: micro_solve(): jnp.dot(misfit.astype(jnp.bfloat16), precond, preferred_element_type=jnp....]
    pallas_call x0 -> x1, Pallas kernels: none -> 14.1 us  [micro_solve(): pl.pallas_call(micro_kernel, grid=(points // tile,), out_shape=jax.ShapeD...]
    pad x0 -> x4, local copies, waits for them, and re-layouts: none -> 2.09 us  [the longest x1 0.68 us: micro_solve(): force = jnp.pad(forcing.T, ((0, 0), (0, 2)))]
    unnamed x20 -> x33, local copies, waits for them, and re-layouts: 3.93 us -> 5.11 us
where the time goes in v2:
time: 131 us
  Pallas kernels  63.6 us (49%)
  starting transfers between devices  24.1 us (18%)
  local copies, waits for them, and re-layouts  19.1 us (15%)
  waiting for transfers between devices  18 us (14%)
  other arithmetic  3.46 us (3%)
  between operations  2.4 us (2%)
    pallas_call x1, Pallas kernels, conjugate_gradients(): pl.pallas_call(body, out_shape=[jax.ShapeDtypeStruct(load.shape, jnp.floa...  49.5 us
    pallas_call x1, Pallas kernels, micro_solve(): pl.pallas_call(micro_kernel, grid=(points // tile,), out_shape=jax.ShapeD...  14.1 us
    all_to_all x1, waiting for transfers between devices, shards(): lax.all_to_all(rows, 'micro', split_axis=1, concat_axis=1, tiled=True)  9.62 us
    ppermute x2, starting transfers between devices, with_halo(): lax.ppermute(lax.slice_in_dim(block, block.shape[dim] - width, None, axis...  6.32 us
    all_to_all x1, starting transfers between devices, shards(): got = lax.all_to_all(send, 'micro', split_axis=1, concat_axis=1, tiled=True)  5.91 us
    ppermute x2, starting transfers between devices, passed_along(): lax.ppermute(value, axis, [(source, source + steps) for source in range(i...  5.85 us
    unnamed x33, local copies, waits for them, and re-layouts  5.11 us
    all_to_all x1, waiting for transfers between devices, shards(): got = lax.all_to_all(send, 'micro', split_axis=1, concat_axis=1, tiled=True)  3.89 us
  transfers between devices with their start and end apart: 8, of which 5 were waited for; matrix products, arithmetic and copies ran while one was open for 5% of the time, Pallas kernels for 0%

profile of v2, /device:TPU:0, one launch (start us, length us, event | category | flops | bytes accessed | tf_op | source)
XLA Modules:
  0.0 130.6 jit_solution(6315789215589275761)
XLA Ops:
  0.6 0.7 fusion.16
  1.4 4.9 %collective-permute-start = (f32[3,1,2,256]{3,2,1,0:T(2,128)S(1)}, f32[3,1,2,256]{3,2,1,0:T(2,128)S(1)}, u32[]{:S(2)}, u32[]{:S(2)}) collective-permute-start(f32[3,1,2,256]{3,2,1,0:T(2,128)S(1)} %get-tuple-element.28), channel_id=1, source_target_pairs={{0,8},{8,16},{16,24},{1,9},{9,17},{17,25},{2,10},{10,18},{18,26},{... | collective-permute-start | bytes 18440 | tf_op jit(solution)/shard_map/ppermute | solution.py:27
  6.2 1.3 collective-permute-start.1
  7.6 2.3 %reduce-window.6 = s32[8,8,128]{2,1,0:T(8,128)S(1)} reduce-window(s32[8,8,128]{2,1,0:T(8,128)S(1)} %fusion.14, s32[]{:T(128)} %constant.11.clone.1), window={size=1x1x128 pad=0_0x0_0x127_0}, to_apply=%region_0.1 | reduce-window | flops 1040384 | bytes 65540 | tf_op jit(solution)/shard_map/reduce-window
  10.4 0.7 copy-done.3
  12.6 0.6 copy-done.1
  13.3 1.5 %collective-permute-start.2 = (f32[3,4,1,256]{3,2,1,0:T(1,128)S(1)}, f32[3,4,1,256]{3,2,1,0:T(1,128)S(1)}, u32[]{:S(2)}, u32[]{:S(2)}) collective-permute-start(f32[3,4,1,256]{3,2,1,0:T(1,128)S(1)} %get-tuple-element.4), channel_id=1, source_target_pairs={{0,1},{1,2},{2,3},{3,4},{4,5},{5,6},{6,7},{8,9},{9,10},{10,11},{11... | collective-permute-start | bytes 36872 | tf_op jit(solution)/shard_map/ppermute | solution.py:27
  14.7 1.3 collective-permute-start.3
  16.1 0.7 copy.38.coef_ref
  16.9 2.5 %collective-permute-done.3 = f32[3,4,1,256]{3,2,1,0:T(1,128)S(1)} collective-permute-done((f32[3,4,1,256]{3,2,1,0:T(1,128)S(1)}, f32[3,4,1,256]{3,2,1,0:T(1,128)S(1)}, u32[]{:S(2)}, u32[]{:S(2)}) %collective-permute-start.3) | collective-permute-done | bytes 12320 | tf_op jit(solution)/shard_map/ppermute | solution.py:30
  20.3 3.3 %scatter_custom_fusion = f32[8,2048]{0,1:T(8,128)S(1)} fusion(s32[1024]{0:T(1024)S(1)} %bitcast.71, f32[1024,8]{1,0:T(8,128)S(1)} %copy.35, f32[]{:T(128)} %constant.12.clone.1), kind=kCustom, calls=%fused_computation.2 | custom fusion | bytes 65540 | tf_op jit(solution)/shard_map/scatter | solution.py:530
  23.6 0.9 copy.36
  24.6 5.9 %all-to-all-start = ((f32[8,8,256]{2,0,1:T(8,128)}), f32[8,8,256]{2,0,1:T(8,128)S(1)}, u32[]{:S(2)}, u32[]{:S(2)}) async-start(f32[8,8,256]{2,0,1:T(8,128)} %copy.36), calls=%async_computation | async-start | bytes 131072 | tf_op jit(solution)/shard_map/all_to_all | solution.py:533
  30.6 0.6 pad.33.product_ref
  31.2 0.7 pad.31.force_ref
  31.9 0.6 pad.32.couple_ref
  32.5 3.9 %all-to-all-done = f32[8,8,256]{2,0,1:T(8,128)S(1)} async-done(((f32[8,8,256]{2,0,1:T(8,128)}), f32[8,8,256]{2,0,1:T(8,128)S(1)}, u32[]{:S(2)}, u32[]{:S(2)}) %all-to-all-start) | async-done | bytes 65568 | tf_op jit(solution)/shard_map/all_to_all | solution.py:533
  36.4 0.6 copy-done
  37.0 14.1 %micro_solve.1 = f32[27,2048]{1,0:T(8,128)} custom-call(f32[8,2048]{1,0:T(8,128)} %bitcast.64, bf16[512,512]{1,0:T(8,128)(2,1)} %bitcast.61, bf16[512,512]{1,0:T(8,128)(2,1)} %bitcast.62, bf16[512,8]{1,0:T(8,128)(2,1)} %pad.31.force_ref, bf16[32,512]{1,0:T(8,128)(2,1)} %pad.32.couple_ref, bf16[32,512]{1,0:T(8,128)(2,1)} %pad.33.product_ref, ...), custom_call_target="tpu_custom_call" | custom-call | tf_op jit(solution)/shard_map/micro_solve/pallas_call | solution.py:169
  51.1 1.0 copy.44
  52.1 0.8 copy.39
  52.9 3.4 %all-to-all-start.1 = ((f32[27,8,256]{2,0,1:T(8,128)}), f32[27,8,256]{2,0,1:T(8,128)S(1)}, u32[]{:S(2)}, u32[]{:S(2)}) async-start(f32[27,8,256]{2,0,1:T(8,128)} %copy.39), calls=%async_computation.1 | async-start | bytes 524288 | tf_op jit(solution)/shard_map/all_to_all | solution.py:544
  56.3 9.6 %all-to-all-done.1 = f32[27,8,256]{2,0,1:T(8,128)S(1)} async-done(((f32[27,8,256]{2,0,1:T(8,128)}), f32[27,8,256]{2,0,1:T(8,128)S(1)}, u32[]{:S(2)}, u32[]{:S(2)}) %all-to-all-start.1) | async-done | bytes 221216 | tf_op jit(solution)/shard_map/all_to_all | solution.py:544
  66.3 2.8 %gather_fusion = f32[1024,27]{1,0:T(8,128)S(1)} fusion(f32[27,2048]{0,1:T(8,128)S(1)} %bitcast.56, s32[1024]{0:T(1024)S(1)} %broadcast_clamp_fusion), kind=kCustom, calls=%fused_computation | custom fusion | bytes 225280 | tf_op jit(solution)/shard_map/jit(_take)/gather | solution.py:545
  69.4 4.6 %collective-permute-start.4 = (f32[27,1,2,256]{3,2,1,0:T(2,128)S(1)}, f32[27,1,2,256]{3,2,1,0:T(2,128)S(1)}, u32[]{:S(2)}, u32[]{:S(2)}) collective-permute-start(f32[27,1,2,256]{3,2,1,0:T(2,128)S(1)} %slice.201), channel_id=1, source_target_pairs={{0,8},{8,16},{16,24},{1,9},{9,17},{17,25},{2,10},{10,18},{18,26},{... | collective-permute-start | bytes 165896 | tf_op jit(solution)/shard_map/ppermute | solution.py:38
  73.9 1.8 %collective-permute-done.4 = f32[27,1,2,256]{3,2,1,0:T(2,128)S(1)} collective-permute-done((f32[27,1,2,256]{3,2,1,0:T(2,128)S(1)}, f32[27,1,2,256]{3,2,1,0:T(2,128)S(1)}, u32[]{:S(2)}, u32[]{:S(2)}) %collective-permute-start.4) | collective-permute-done | bytes 55328 | tf_op jit(solution)/shard_map/ppermute | solution.py:38
  75.8 1.3 collective-permute-start.5
  77.2 0.6 reshape.88.refs_0_
  78.2 0.9 reshape.92.refs_1_
  79.2 49.5 %conjugate_gradients.1 = (f32[3,2,2,256]{3,2,1,0:T(2,128)}, f32[3,2,2,256]{3,2,1,0:T(2,128)}) custom-call(f32[3,16,256]{2,1,0:T(8,128)} %reshape.88.refs_0_, f32[27,16,256]{2,1,0:T(8,128)} %reshape.92.refs_1_), custom_call_target="tpu_custom_call" | custom-call | tf_op jit(solution)/shard_map/conjugate_gradients/pallas_call | solution.py:476
  128.7 1.3 %copy.57 = f32[3,2,2,256]{3,2,1,0:T(2,128)} copy(f32[3,2,2,256]{3,2,1,0:T(2,128)} %get-tuple-element.33) | data formatting | bytes 24576
  130.0 0.6 copy.58
  (66 shorter events, 2.9 us)
Async XLA Ops:
  0.6 6.9 %copy-start.7 = (s32[1,1,1024]{2,1,0:T(1,128)S(1)}, s32[1,1,1024]{2,1,0:T(1,128)}, u32[]{:S(2)}) copy-start(s32[1,1,1024]{2,1,0:T(1,128)} %param.17) | copy-start | bytes 12292
  1.4 11.2 %collective-permute-start = (f32[3,1,2,256]{3,2,1,0:T(2,128)S(1)}, f32[3,1,2,256]{3,2,1,0:T(2,128)S(1)}, u32[]{:S(2)}, u32[]{:S(2)}) collective-permute-start(f32[3,1,2,256]{3,2,1,0:T(2,128)S(1)} %get-tuple-element.28), channel_id=1, source_target_pairs={{0,8},{8,16},{16,24},{1,9},{9,17},{17,25},{2,10},{10,18},{18,26},{... | collective-permute-start | bytes 18440 | tf_op jit(solution)/shard_map/ppermute | solution.py:27
  6.2 1.3 %copy-start.2 = (s32[1,1,1024,1]{2,3,1,0:T(1,128)S(1)}, s32[1,1,1024,1]{2,3,1,0:T(1,128)}, u32[]{:S(2)}) copy-start(s32[1,1,1024,1]{2,3,1,0:T(1,128)} %param.16) | copy-start | bytes 12292
  6.2 7.0 %collective-permute-start.1 = (f32[3,1,2,256]{3,2,1,0:T(2,128)S(1)}, f32[3,1,2,256]{3,2,1,0:T(2,128)S(1)}, u32[]{:S(2)}, u32[]{:S(2)}) collective-permute-start(f32[3,1,2,256]{3,2,1,0:T(2,128)S(1)} %get-tuple-element.27), channel_id=1, source_target_pairs={{8,0},{16,8},{24,16},{9,1},{17,9},{25,17},{10,2},{18,10},{26,18},{... | collective-permute-start | bytes 18440 | tf_op jit(solution)/shard_map/ppermute | solution.py:30
  10.4 0.7 copy-start.3
  11.1 1.4 %copy-start.8 = (f32[32]{0:T(128)S(1)}, f32[32]{0:T(128)}, u32[]{:S(2)}) copy-start(f32[32]{0:T(128)} %constant.32.clone) | copy-start | bytes 388
  11.2 1.4 %copy-start.9 = (f32[32]{0:T(128)S(1)}, f32[32]{0:T(128)}, u32[]{:S(2)}) copy-start(f32[32]{0:T(128)} %constant.33.clone) | copy-start | bytes 388
  11.2 1.4 %copy-start.10 = (f32[32]{0:T(128)S(1)}, f32[32]{0:T(128)}, u32[]{:S(2)}) copy-start(f32[32]{0:T(128)} %constant.34.clone) | copy-start | bytes 388
  11.2 1.4 %copy-start.11 = (f32[32]{0:T(128)S(1)}, f32[32]{0:T(128)}, u32[]{:S(2)}) copy-start(f32[32]{0:T(128)} %constant.31.clone) | copy-start | bytes 388
  12.5 0.7 copy-start.1
  13.3 3.7 %collective-permute-start.2 = (f32[3,4,1,256]{3,2,1,0:T(1,128)S(1)}, f32[3,4,1,256]{3,2,1,0:T(1,128)S(1)}, u32[]{:S(2)}, u32[]{:S(2)}) collective-permute-start(f32[3,4,1,256]{3,2,1,0:T(1,128)S(1)} %get-tuple-element.4), channel_id=1, source_target_pairs={{0,1},{1,2},{2,3},{3,4},{4,5},{5,6},{6,7},{8,9},{9,10},{10,11},{11... | collective-permute-start | bytes 36872 | tf_op jit(solution)/shard_map/ppermute | solution.py:27
  14.7 4.7 %collective-permute-start.3 = (f32[3,4,1,256]{3,2,1,0:T(1,128)S(1)}, f32[3,4,1,256]{3,2,1,0:T(1,128)S(1)}, u32[]{:S(2)}, u32[]{:S(2)}) collective-permute-start(f32[3,4,1,256]{3,2,1,0:T(1,128)S(1)} %get-tuple-element.5), channel_id=1, source_target_pairs={{1,0},{2,1},{3,2},{4,3},{5,4},{6,5},{7,6},{9,8},{10,9},{11,10},{12... | collective-permute-start | bytes 36872 | tf_op jit(solution)/shard_map/ppermute | solution.py:30
  16.0 0.7 copy-start.6
  24.6 11.8 %all-to-all-start = ((f32[8,8,256]{2,0,1:T(8,128)}), f32[8,8,256]{2,0,1:T(8,128)S(1)}, u32[]{:S(2)}, u32[]{:S(2)}) async-start(f32[8,8,256]{2,0,1:T(8,128)} %copy.36), calls=%async_computation | async-start | bytes 131072 | tf_op jit(solution)/shard_map/all_to_all | solution.py:533
  36.4 0.6 copy-start
  52.9 13.1 %all-to-all-start.1 = ((f32[27,8,256]{2,0,1:T(8,128)}), f32[27,8,256]{2,0,1:T(8,128)S(1)}, u32[]{:S(2)}, u32[]{:S(2)}) async-start(f32[27,8,256]{2,0,1:T(8,128)} %copy.39), calls=%async_computation.1 | async-start | bytes 524288 | tf_op jit(solution)/shard_map/all_to_all | solution.py:544
  69.4 7.8 %copy-start.5 = (f32[3,2,2,256]{3,2,1,0:T(2,128)S(1)}, f32[3,2,2,256]{3,2,1,0:T(2,128)}, u32[]{:S(2)}) copy-start(f32[3,2,2,256]{3,2,1,0:T(2,128)} %param.15) | copy-start | bytes 36868
  69.4 6.3 %collective-permute-start.4 = (f32[27,1,2,256]{3,2,1,0:T(2,128)S(1)}, f32[27,1,2,256]{3,2,1,0:T(2,128)S(1)}, u32[]{:S(2)}, u32[]{:S(2)}) collective-permute-start(f32[27,1,2,256]{3,2,1,0:T(2,128)S(1)} %slice.201), channel_id=1, source_target_pairs={{0,8},{8,16},{16,24},{1,9},{9,17},{17,25},{2,10},{10,18},{18,26},{... | collective-permute-start | bytes 165896 | tf_op jit(solution)/shard_map/ppermute | solution.py:38
  75.8 2.2 %collective-permute-start.5 = (f32[27,3,1,256]{3,2,1,0:T(1,128)S(1)}, f32[27,3,1,256]{3,2,1,0:T(1,128)S(1)}, u32[]{:S(2)}, u32[]{:S(2)}) collective-permute-start(f32[27,3,1,256]{3,2,1,0:T(1,128)S(1)} %pad_maximum_fusion), channel_id=1, source_target_pairs={{0,1},{1,2},{2,3},{3,4},{4,5},{5,6},{6,7},{8,9},{9,10},{10,11},{11... | collective-permute-start | bytes 248840 | tf_op jit(solution)/shard_map/ppermute | solution.py:38
  128.7 1.3 %copy-start.4 = (f32[3,2,2,256]{3,2,1,0:T(2,128)S(1)}, f32[3,2,2,256]{3,2,1,0:T(2,128)}, u32[]{:S(2)}) copy-start(f32[3,2,2,256]{3,2,1,0:T(2,128)} %get-tuple-element.34) | copy-start | bytes 36868
